TPU v7x, 128 devices: a whole 4x4x4 slice. The times are simulated.
128 devices in a mesh: dp: 16 (over x_lo, y, core), tensor: 8 (over x_hi, z).
Axes of the slice: x: 4 (x_hi: 2, x_lo: 2; x = x_hi * 2 + x_lo), y: 4, z: 4, core: 2. Of those that a mesh axis runs over, the one named last changes fastest.
Arguments:
- block_input: bfloat16 [32768, 768], P(('dp', 'tensor')), may hold values from -6 to 6
- w_value: bfloat16 [768, 768], replicated, may hold values from -0.21875 to 0.21875
- b_value: bfloat16 [768], replicated, may hold values from -2 to 2
- conv_kernel: bfloat16 [65, 768], replicated, may hold values from -0.75 to 0.75
- w_out: bfloat16 [768, 768], replicated, may hold values from -0.21875 to 0.21875
- b_out: bfloat16 [768], replicated, may hold values from -2 to 2
- gain_attn: bfloat16 [768], replicated, may hold values from 0.5 to 1.5
- shift_attn: bfloat16 [768], replicated, may hold values from -2 to 2
- w_up: bfloat16 [768, 3072], P(None, 'tensor'), may hold values from -0.21875 to 0.21875
- b_up: bfloat16 [3072], P('tensor'), may hold values from -2 to 2
- w_down: bfloat16 [3072, 768], P('tensor'), may hold values from -0.109375 to 0.109375
- b_down: bfloat16 [768], replicated, may hold values from -2 to 2
- gain_ffn: bfloat16 [768], replicated, may hold values from 0.5 to 1.5
- shift_ffn: bfloat16 [768], replicated, may hold values from -2 to 2
- query_codes: int32 [32768, 384], P(('dp', 'tensor')), may hold values from 0 to 255
- key_codes: int32 [32768, 384], P(('dp', 'tensor')), may hold values from 0 to 255
- key_live: int32 [32768], P(('dp', 'tensor')), may hold values 0 or 1
- seq_lengths: int32 [128, 4], P(('dp', 'tensor')), may hold values from 1 to 128, 256 in all within a row
- out_grad: bfloat16 [32768, 768], P(('dp', 'tensor')), may hold values from -6 to 6
Outputs:
- block_output: bfloat16 [32768, 768], P(('dp', 'tensor'))
- input_grad: float32 [32768, 768], P(('dp', 'tensor'))
- grad_w_value: float32 [768, 768], replicated
- grad_b_value: float32 [768], replicated
- grad_conv_kernel: float32 [65, 768], replicated
- grad_w_out: float32 [768, 768], replicated
- grad_b_out: float32 [768], replicated
- grad_gain_attn: float32 [768], replicated
- grad_shift_attn: float32 [768], replicated
- grad_w_up: float32 [768, 3072], P(None, 'tensor')
- grad_b_up: float32 [3072], P('tensor')
- grad_w_down: float32 [3072, 768], P('tensor')
- grad_b_down: float32 [768], replicated
- grad_gain_ffn: float32 [768], replicated
- grad_shift_ffn: float32 [768], replicated
Inputs may be any that keep to these rules, and one draw needn't show every extreme that they name: `seq_lengths`: each item's lengths sum to 256; the longest is 128. `key_live`: 1 marks a live key, 0 a padded one. `query_codes`: column h * 32 + s holds head h's code in hash set s. `key_codes`: column h * 32 + s holds head h's code in hash set s.
All inputs are finite; a program needn't handle non-finite values. No bound on the sum of `key_live` on one device may be relied on, other than what follows from the above.
Results may differ from a plain program's by a relative error of at most 0.02.
Values may be sent and summed in bfloat16 or wider, within the bound.
No kernel may reach another device: no remote copies, remote signals or barrier semaphores. Data moves between devices by JAX's collectives and lax.ppermute only.
A program may use at most 128 MiB of HBM per device.

v0:
```python
from functools import partial
import jax
import jax.numpy as jnp
from jax import lax
from jax.sharding import PartitionSpec as P

HEADS = 12
SETS = 32
BUCKETS = 256


def dot_last(former, latter):
    return lax.dot_general(
        former, latter, (((1,), (1,)), ((), ())), preferred_element_type=jnp.float32
    )


def dot_first(former, latter):
    return lax.dot_general(
        former, latter, (((0,), (0,)), ((), ())), preferred_element_type=jnp.float32
    )


def layer_norm(residual, gain_vec, shift_vec):
    average = jnp.mean(residual, axis=-1, keepdims=True)
    centred = residual - average
    variance = jnp.mean(centred * centred, axis=-1, keepdims=True)
    return centred * lax.rsqrt(variance + 1e-05) * gain_vec + shift_vec


def head_norm(mixed, head_count, head_dim):
    grouped = mixed.reshape(mixed.shape[0], head_count, head_dim)
    scaling = lax.rsqrt(jnp.mean(grouped * grouped, axis=-1, keepdims=True) + 1e-06)
    return (grouped * scaling).reshape(mixed.shape)


def gelu_exact(pre_act):
    return jax.nn.gelu(pre_act, approximate=False)


def depth_conv(values, kernel, segment):
    taps = kernel.shape[0]
    margin = taps // 2
    length = values.shape[0]
    padded = jnp.pad(values, ((margin, margin), (0, 0)))
    seg_padded = jnp.pad(segment, (margin, margin), constant_values=-1)
    running = jnp.zeros_like(values)
    for offset in range(taps):
        joined = (seg_padded[offset : offset + length] == segment).astype(jnp.float32)[:, None]
        running = running + padded[offset : offset + length] * joined * kernel[offset][None, :]
    return running


def conv_back(grad_out, values, kernel, segment):
    taps = kernel.shape[0]
    margin = taps // 2
    length = values.shape[0]
    padded = jnp.pad(values, ((margin, margin), (0, 0)))
    grad_padded = jnp.pad(grad_out, ((margin, margin), (0, 0)))
    seg_padded = jnp.pad(segment, (margin, margin), constant_values=-1)
    value_grad = jnp.zeros_like(values)
    tap_rows = []
    for offset in range(taps):
        joined = (seg_padded[offset : offset + length] == segment).astype(jnp.float32)[:, None]
        tap_rows.append(jnp.sum(grad_out * joined * padded[offset : offset + length], axis=0))
        mirror = 2 * margin - offset
        back_joined = (seg_padded[mirror : mirror + length] == segment).astype(jnp.float32)[:, None]
        value_grad = (
            value_grad
            + grad_padded[mirror : mirror + length] * back_joined * kernel[offset][None, :]
        )
    return (value_grad, jnp.stack(tap_rows, axis=0))


def body(
    block_input,
    w_value,
    b_value,
    conv_kernel,
    w_out,
    b_out,
    gain_attn,
    shift_attn,
    w_up,
    b_up,
    w_down,
    b_down,
    gain_ffn,
    shift_ffn,
    query_codes,
    key_codes,
    key_live,
    seq_lengths,
    out_grad,
):
    length = block_input.shape[0]
    model_width = block_input.shape[1]
    head_dim = model_width // HEADS
    live_keys = key_live.astype(jnp.float32)[:, None]
    seq_ends = jnp.cumsum(seq_lengths[0], dtype=jnp.int32)
    positions = jnp.arange(length, dtype=jnp.int32)
    segment = jnp.sum(
        (seq_ends[None, :] <= positions[:, None]).astype(jnp.int32), axis=1, dtype=jnp.int32
    )
    query_heads = query_codes.reshape(length, HEADS, SETS).transpose(1, 0, 2)
    key_heads = key_codes.reshape(length, HEADS, SETS).transpose(1, 0, 2)
    joined = (segment[:, None] == segment[None, :]).astype(jnp.float32)
    bucket_ids = jnp.arange(BUCKETS, dtype=jnp.int32)

    def head_counts(pair):
        query_set, key_set = pair
        query_hot = (
            (query_set[:, :, None] == bucket_ids[None, None, :])
            .astype(jnp.bfloat16)
            .reshape(length, SETS * BUCKETS)
        )
        key_hot = (
            (key_set[:, :, None] == bucket_ids[None, None, :])
            .astype(jnp.bfloat16)
            .reshape(length, SETS * BUCKETS)
        )
        counts = dot_last(query_hot, key_hot)
        return (counts * joined / SETS).astype(jnp.bfloat16)

    collide = lax.map(head_counts, (query_heads, key_heads))
    kernel_f = conv_kernel.astype(jnp.float32)
    value_pre = jnp.dot(block_input, w_value, preferred_element_type=jnp.float32) + b_value.astype(
        jnp.float32
    )
    values = value_pre.astype(jnp.bfloat16)
    masked = values.astype(jnp.float32) * live_keys
    masked_low = masked.astype(jnp.bfloat16)
    mixed = jnp.einsum(
        "hij,jhd->ihd",
        collide,
        masked_low.reshape(length, HEADS, head_dim),
        preferred_element_type=jnp.float32,
    ).reshape(length, model_width)
    normed, norm_back = jax.vjp(partial(head_norm, head_count=HEADS, head_dim=head_dim), mixed)
    context = (normed + depth_conv(masked, kernel_f, segment)).astype(jnp.bfloat16)
    attended = jnp.dot(context, w_out, preferred_element_type=jnp.float32) + b_out.astype(
        jnp.float32
    )
    first, first_back = jax.vjp(
        layer_norm,
        block_input.astype(jnp.float32) + attended,
        gain_attn.astype(jnp.float32),
        shift_attn.astype(jnp.float32),
    )
    first_low = first.astype(jnp.bfloat16)
    gathered = lax.all_gather(first_low, "tensor", axis=0, tiled=True)
    upper = jnp.dot(gathered, w_up, preferred_element_type=jnp.float32) + b_up.astype(jnp.float32)
    active_f, gelu_back = jax.vjp(gelu_exact, upper)
    active = active_f.astype(jnp.bfloat16)
    branch = lax.psum_scatter(
        jnp.dot(active, w_down, preferred_element_type=jnp.float32).astype(jnp.bfloat16),
        "tensor",
        scatter_dimension=0,
        tiled=True,
    ).astype(jnp.float32) + b_down.astype(jnp.float32)
    block_output, second_back = jax.vjp(
        layer_norm, first + branch, gain_ffn.astype(jnp.float32), shift_ffn.astype(jnp.float32)
    )
    grad_second, grad_gain_ffn, grad_shift_ffn = second_back(out_grad.astype(jnp.float32))
    branch_grad = grad_second.astype(jnp.bfloat16)
    grad_b_down = jnp.sum(branch_grad.astype(jnp.float32), axis=0)
    grad_rows_all = lax.all_gather(branch_grad, "tensor", axis=0, tiled=True)
    active_grad = dot_last(grad_rows_all, w_down)
    grad_w_down = dot_first(active, grad_rows_all)
    upper_grad = gelu_back(active_grad)[0].astype(jnp.bfloat16)
    grad_w_up = dot_first(gathered, upper_grad)
    grad_b_up = jnp.sum(upper_grad.astype(jnp.float32), axis=0)
    first_grad_ffn = lax.psum_scatter(
        dot_last(upper_grad, w_up).astype(jnp.bfloat16), "tensor", scatter_dimension=0, tiled=True
    ).astype(jnp.float32)
    first_grad = grad_second + first_grad_ffn
    resid_grad, grad_gain_attn, grad_shift_attn = first_back(first_grad)
    attended_grad = resid_grad.astype(jnp.bfloat16)
    grad_b_out = jnp.sum(attended_grad.astype(jnp.float32), axis=0)
    grad_w_out = dot_first(context, attended_grad)
    context_grad = dot_last(attended_grad, w_out)
    mixed_grad = norm_back(context_grad)[0].astype(jnp.bfloat16)
    conv_value_grad, grad_kernel = conv_back(context_grad, masked, kernel_f, segment)
    masked_att = jnp.einsum(
        "hij,ihd->jhd",
        collide,
        mixed_grad.reshape(length, HEADS, head_dim),
        preferred_element_type=jnp.float32,
    ).reshape(length, model_width)
    value_grad = ((masked_att + conv_value_grad) * live_keys).astype(jnp.bfloat16)
    grad_b_value = jnp.sum(value_grad.astype(jnp.float32), axis=0)
    grad_w_value = dot_first(block_input, value_grad)
    input_grad = resid_grad + dot_last(value_grad, w_value)
    grad_w_up, grad_w_down, grad_b_up = (
        lax.psum(grad_w_up.astype(jnp.bfloat16), "dp").astype(jnp.float32),
        lax.psum(grad_w_down.astype(jnp.bfloat16), "dp").astype(jnp.float32),
        lax.psum(grad_b_up.astype(jnp.bfloat16), "dp").astype(jnp.float32),
    )
    (
        grad_w_value,
        grad_b_value,
        grad_kernel,
        grad_w_out,
        grad_b_out,
        grad_gain_attn,
        grad_shift_attn,
        grad_b_down,
        grad_gain_ffn,
        grad_shift_ffn,
    ) = lax.psum(
        (
            grad_w_value,
            grad_b_value,
            grad_kernel,
            grad_w_out,
            grad_b_out,
            grad_gain_attn,
            grad_shift_attn,
            grad_b_down,
            grad_gain_ffn,
            grad_shift_ffn,
        ),
        ("dp", "tensor"),
    )
    return (
        block_output.astype(jnp.bfloat16),
        input_grad,
        grad_w_value,
        grad_b_value,
        grad_kernel,
        grad_w_out,
        grad_b_out,
        grad_gain_attn,
        grad_shift_attn,
        grad_w_up,
        grad_b_up,
        grad_w_down,
        grad_b_down,
        grad_gain_ffn,
        grad_shift_ffn,
    )


def solution(mesh):
    return jax.shard_map(
        body,
        mesh=mesh,
        in_specs=(
            P(("dp", "tensor"), None),
            P(),
            P(),
            P(),
            P(),
            P(),
            P(),
            P(),
            P(None, "tensor"),
            P("tensor"),
            P("tensor", None),
            P(),
            P(),
            P(),
            P(("dp", "tensor"), None),
            P(("dp", "tensor"), None),
            P(("dp", "tensor")),
            P(("dp", "tensor"), None),
            P(("dp", "tensor"), None),
        ),
        out_specs=(
            P(("dp", "tensor"), None),
            P(("dp", "tensor"), None),
            P(),
            P(),
            P(),
            P(),
            P(),
            P(),
            P(),
            P(None, "tensor"),
            P("tensor"),
            P("tensor", None),
            P(),
            P(),
            P(),
        ),
        check_vma=False,
    )
```

profile of v0, /device:TPU:1, one launch (start us, length us, event | category | flops | bytes accessed | tf_op | source)
XLA Modules:
  0.0 701.4 jit_solution(10940862884612107198)
XLA Ops:
  17.3 43.1 %while.12 = (s32[]{:T(128)}, bf16[12,256,256]{2,1,0:T(8,128)(2,1)}, s32[12,256,32]{1,2,0:T(8,128)S(1)}, s32[12,256,32]{1,2,0:T(8,128)S(1)}, s32[256]{0:T(256)S(1)}, /*index=5*/s32[]{:T(128)}) while((s32[]{:T(128)}, bf16[12,256,256]{2,1,0:T(8,128)(2,1)}, s32[12,256,32]{1,2,0:T(8,128)S(1)}, s32[12,256,32]{1,2,0:T(8,128)S(1)}, ...), condition=%wide.region_3.4_spmd.clone.clone, body=%wide.region_2.3_spmd.clone.clone.sunk | while | flops 1078198272 | bytes 330313 | solution.py:125
  17.4 3.6 fusion.266
  21.0 3.6 fusion.266
  24.6 3.6 fusion.266
  28.1 3.6 fusion.266
  35.3 3.6 fusion.266
  42.5 3.6 fusion.266
  46.1 3.6 fusion.266
  53.3 3.6 fusion.266
  66.3 11.6 %add_convert_fusion.2 = bf16[256,768]{1,0:T(8,128)(2,1)S(1)} fusion(f32[256,768]{1,0:T(8,128)S(1)} %copy.51, f32[256,768]{1,0:T(8,128)S(1)} %get-tuple-element.368, f32[768]{0:T(1024)} %get-tuple-element.198, f32[256]{0:T(256)} %get-tuple-element.366, f32[768]{0:T(1024)} %get-tuple-element.199, f32[256]{0:T(256)} %get-tuple-element.365, ...), kind=kLoop, calls=%fused_computation.456 | loop fusion | flops 38338560 | bytes 2231296 | tf_op jit(solution)/shard_map/convert_element_type | solution.py:140
  83.6 11.4 %reduce-scatter.3.cloned.1.call-start = ((), (), s32[]{:S(2)}) async-start(), calls=%async_computation.3 | async-start | bytes 3538944 | tf_op jit(solution)/shard_map/reduce_scatter | solution.py:155
  96.2 53.2 %all-gather.3.cloned.1.call-done = bf16[2048,768]{1,0:T(8,128)(2,1)} async-done(((bf16[256,768]{1,0:T(8,128)(2,1)}), bf16[2048,768]{1,0:T(8,128)(2,1)}) %all-gather.3.cloned.1.call-update) | async-done | bytes 3145744 | tf_op jit(solution)/shard_map/all_gather | solution.py:151
  149.4 11.6 %multiply_convert_fusion = (bf16[2048,384]{1,0:T(8,128)(2,1)S(1)}, f32[2048,384]{1,0:T(8,128)}, f32[2048,384]{1,0:T(8,128)}) fusion(f32[384]{0:T(512)} %convert_element_type.529, bf16[2048,768]{1,0:T(8,128)(2,1)} %all-gather.3.cloned.1.call-done, bf16[768,384]{1,0:T(8,128)(2,1)} %param.29), kind=kOutput, calls=%fused_computation.148 | convolution fusion | flops 1259864064 | bytes 11601408 | tf_op jit(solution)/shard_map/dot_general | solution.py:152
  169.5 72.7 %reduce-scatter.3.cloned.1.call-done = bf16[256,768]{1,0:T(8,128)(2,1)} async-done(((bf16[2048,768]{1,0:T(8,128)(2,1)}), bf16[256,768]{1,0:T(8,128)(2,1)}) %reduce-scatter.3.cloned.1.call-update) | async-done | bytes 393232 | tf_op jit(solution)/shard_map/reduce_scatter | solution.py:155
  249.4 62.5 %all-gather.5.cloned.1.call-done = bf16[2048,768]{1,0:T(8,128)(2,1)} async-done(((bf16[256,768]{1,0:T(8,128)(2,1)}), bf16[2048,768]{1,0:T(8,128)(2,1)}) %all-gather.5.cloned.1.call-update) | async-done | bytes 3145744 | tf_op jit(solution)/shard_map/all_gather | solution.py:167
  311.9 7.3 %fusion.230 = (bf16[384]{0:T(512)(128)(2,1)}, bf16[2048,384]{1,0:T(8,128)(2,1)S(1)}) fusion(f32[2048,384]{1,0:T(8,128)} %get-tuple-element.299, f32[2048,384]{1,0:T(8,128)} %get-tuple-element.373, bf16[2048,768]{1,0:T(8,128)(2,1)} %all-gather.5.cloned.1.call-done, bf16[384,768]{1,0:T(8,128)(2,1)} %param.31), kind=kOutput, calls=%fused_computation.674 | convolution fusion | flops 1219755648 | bytes 11600640 | tf_op jit(solution)/shard_map/dot_general | solution.py:13
  324.0 4.8 convolution_convert_fusion.2
  331.5 69.1 %reduce-scatter.5.cloned.1.call-done = bf16[256,768]{1,0:T(8,128)(2,1)} async-done(((bf16[2048,768]{1,0:T(8,128)(2,1)}), bf16[256,768]{1,0:T(8,128)(2,1)}) %reduce-scatter.5.cloned.1.call-update) | async-done | bytes 393232 | tf_op jit(solution)/shard_map/reduce_scatter | solution.py:173
  451.9 5.8 stack.263
  457.7 11.7 %convert_reduce_fusion.3 = (f32[768]{0:T(1024)S(1)}, bf16[256,768]{1,0:T(8,128)(2,1)S(1)}) fusion(f32[256]{0:T(256)} %copy-done.110, f32[256,768]{1,0:T(8,128)S(1)} %copy.53, f32[768]{0:T(1024)} %get-tuple-element.198, f32[256]{0:T(256)} %get-tuple-element.303, f32[768]{0:T(1024)} %get-tuple-element.199, f32[256]{0:T(256)} %get-tuple-element.321, ...), kind=kLoop, calls=%fused_computation.446 | loop fusion | flops 38927616 | bytes 2235392 | tf_op jit(solution)/shard_map/reduce_sum | solution.py:191
  472.0 28.5 %psum.99 = bf16[384]{0:T(512)(128)(2,1)S(1)} all-reduce(bf16[384]{0:T(512)(128)(2,1)S(1)} %copy-done.120), channel_id=1, replica_groups=mesh['dp'=16,'tensor'=8] {'dp'}, use_global_device_ids=true, to_apply=%region_94.95 | all-reduce | flops 384 | bytes 1536 | tf_op jit(solution)/shard_map/psum | solution.py:197
  501.1 22.6 %all-reduce.11.cloned.1.call-done = (bf16[768,384]{1,0:T(8,128)(2,1)}, bf16[384,768]{1,0:T(8,128)(2,1)}) async-done(((bf16[768,384]{1,0:T(8,128)(2,1)}, bf16[384,768]{1,0:T(8,128)(2,1)}), (bf16[768,384]{1,0:T(8,128)(2,1)}, bf16[384,768]{1,0:T(8,128)(2,1)})) %all-reduce.11.cloned.1.call-update) | async-done | bytes 1179664 | tf_op jit(solution)/shard_map/psum | solution.py:195
  528.0 68.4 %all-reduce.3 = (f32[768]{0:T(1024)}, f32[768]{0:T(1024)}, f32[768]{0:T(1024)}, f32[768]{0:T(1024)}, f32[768]{0:T(1024)}, /*index=5*/f32[768]{0:T(1024)}, f32[768]{0:T(1024)}) all-reduce(f32[768]{0:T(1024)S(1)} %get-tuple-element.290, f32[768]{0:T(1024)S(1)} %copy-done.37, ...), channel_id=1, replica_groups=mesh['dp'=16,'tensor'=8] {'dp','tensor'}, use_global_device_ids=true, to_apply=%region_18.19 | all-reduce | flops 5376 | bytes 43008 | tf_op jit(solution)/shard_map/psum | solution.py:210
  597.9 89.3 %all-reduce.9.cloned.1.call-done = (f32[768,768]{0,1:T(8,128)}, f32[65,768]{1,0:T(8,128)}, f32[768,768]{1,0:T(8,128)}) async-done(((f32[768,768]{0,1:T(8,128)}, f32[65,768]{1,0:T(8,128)}, f32[768,768]{1,0:T(8,128)}), (f32[768,768]{0,1:T(8,128)}, f32[65,768]{1,0:T(8,128)}, f32[768,768]{1,0:T(8,128)})) %all-reduce.9.cloned.1.call-update) | async-done | bytes 4918288 | tf_op jit(solution)/shard_map/psum | solution.py:210
  (413 shorter events, 125.8 us)
Async XLA Ops:
  7.2 53.3 %copy-start = (bf16[768,768]{1,0:T(8,128)(2,1)S(1)}, bf16[768,768]{1,0:T(8,128)(2,1)}, u32[]{:S(2)}) copy-start(bf16[768,768]{1,0:T(8,128)(2,1)} %param.22) | copy-start | bytes 3538948
  7.2 142.2 %all-gather.3.cloned.1.call-start = ((), (), s32[]{:S(2)}) async-start(), calls=%async_computation.2 | async-start | bytes 3538944 | tf_op jit(solution)/shard_map/all_gather | solution.py:151
  17.3 43.1 %copy-start.119 = (s32[256]{0:T(256)S(1)}, s32[256]{0:T(256)}, u32[]{:S(2)}) copy-start(s32[256]{0:T(256)} %param.37) | copy-start | bytes 3076
  17.3 43.1 %copy-start.116 = (bf16[768]{0:T(1024)(128)(2,1)S(1)}, bf16[768]{0:T(1024)(128)(2,1)}, u32[]{:S(2)}) copy-start(bf16[768]{0:T(1024)(128)(2,1)} %param.23) | copy-start | bytes 4612
  17.3 43.1 %copy-start.6 = (bf16[256,768]{1,0:T(8,128)(2,1)S(1)}, bf16[256,768]{1,0:T(8,128)(2,1)}, u32[]{:S(2)}) copy-start(bf16[256,768]{1,0:T(8,128)(2,1)} %param.21) | copy-start | bytes 1179652
  83.6 158.7 %reduce-scatter.3.cloned.1.call-start = ((), (), s32[]{:S(2)}) async-start(), calls=%async_computation.3 | async-start | bytes 3538944 | tf_op jit(solution)/shard_map/reduce_scatter | solution.py:155
  165.6 146.3 %all-gather.5.cloned.1.call-start = ((), (), s32[]{:S(2)}) async-start(), calls=%async_computation.4 | async-start | bytes 3538944 | tf_op jit(solution)/shard_map/all_gather | solution.py:167
  249.3 151.3 %reduce-scatter.5.cloned.1.call-start = ((), (), s32[]{:S(2)}) async-start(), calls=%async_computation.5 | async-start | bytes 3538944 | tf_op jit(solution)/shard_map/reduce_scatter | solution.py:173
  323.9 199.8 %all-reduce.11.cloned.1.call-start = ((), (), s32[]{:S(2)}) async-start(), calls=%async_computation.7 | async-start | bytes 2359296 | tf_op jit(solution)/shard_map/psum | solution.py:195
  331.4 355.7 %all-reduce.9.cloned.1.call-start = ((), (), s32[]{:S(2)}) async-start(), calls=%async_computation.6 | async-start | bytes 9879552 | tf_op jit(solution)/shard_map/psum | solution.py:210
  429.2 21.2 %copy-start.42 = (f32[768]{0:T(1024)S(1)}, f32[768]{0:T(1024)}, u32[]{:S(2)}) copy-start(f32[768]{0:T(1024)} %get-tuple-element.186) | copy-start | bytes 9220
  429.2 21.2 %copy-start.41 = (f32[768]{0:T(1024)S(1)}, f32[768]{0:T(1024)}, u32[]{:S(2)}) copy-start(f32[768]{0:T(1024)} %get-tuple-element.185) | copy-start | bytes 9220
  429.2 21.3 %copy-start.40 = (f32[768]{0:T(1024)S(1)}, f32[768]{0:T(1024)}, u32[]{:S(2)}) copy-start(f32[768]{0:T(1024)} %get-tuple-element.184) | copy-start | bytes 9220
  429.2 21.3 %copy-start.39 = (f32[768]{0:T(1024)S(1)}, f32[768]{0:T(1024)}, u32[]{:S(2)}) copy-start(f32[768]{0:T(1024)} %get-tuple-element.183) | copy-start | bytes 9220
  429.2 21.3 %copy-start.38 = (f32[768]{0:T(1024)S(1)}, f32[768]{0:T(1024)}, u32[]{:S(2)}) copy-start(f32[768]{0:T(1024)} %get-tuple-element.182) | copy-start | bytes 9220
  430.6 38.8 %copy-start.7 = (bf16[256,768]{1,0:T(8,128)(2,1)S(1)}, bf16[256,768]{1,0:T(8,128)(2,1)}, u32[]{:S(2)}) copy-start(bf16[256,768]{1,0:T(8,128)(2,1)} %param.21) | copy-start | bytes 1179652
  471.3 56.7 %copy-start.32 = (f32[768]{0:T(1024)S(1)}, f32[768]{0:T(1024)}, u32[]{:S(2)}) copy-start(f32[768]{0:T(1024)} %get-tuple-element.193) | copy-start | bytes 9220
  471.3 56.7 %copy-start.33 = (f32[768]{0:T(1024)S(1)}, f32[768]{0:T(1024)}, u32[]{:S(2)}) copy-start(f32[768]{0:T(1024)} %get-tuple-element.196) | copy-start | bytes 9220
  471.3 56.7 %copy-start.34 = (f32[768]{0:T(1024)S(1)}, f32[768]{0:T(1024)}, u32[]{:S(2)}) copy-start(f32[768]{0:T(1024)} %get-tuple-element.286) | copy-start | bytes 9220
  471.3 56.7 %copy-start.35 = (f32[768]{0:T(1024)S(1)}, f32[768]{0:T(1024)}, u32[]{:S(2)}) copy-start(f32[768]{0:T(1024)} %get-tuple-element.126) | copy-start | bytes 9220
  471.3 56.7 %copy-start.36 = (f32[768]{0:T(1024)S(1)}, f32[768]{0:T(1024)}, u32[]{:S(2)}) copy-start(f32[768]{0:T(1024)} %get-tuple-element.195) | copy-start | bytes 9220
  471.4 56.7 %copy-start.37 = (f32[768]{0:T(1024)S(1)}, f32[768]{0:T(1024)}, u32[]{:S(2)}) copy-start(f32[768]{0:T(1024)} %get-tuple-element.288) | copy-start | bytes 9220
  471.4 125.1 %copy-start.3 = (f32[256,768]{1,0:T(8,128)S(1)}, f32[256,768]{1,0:T(8,128)}, u32[]{:S(2)}) copy-start(f32[256,768]{1,0:T(8,128)} %copy-done.2) | copy-start | bytes 2359300
  471.4 125.1 %copy-start.115 = (f32[256]{0:T(256)S(1)}, f32[256]{0:T(256)}, u32[]{:S(2)}) copy-start(f32[256]{0:T(256)} %copy-done.114) | copy-start | bytes 3076
  (106 other events, 1160.3 us)
Sparse Core Ops, SparseCore 0:
  83.7 65.6 all-gather.2
  165.7 76.4 reduce-scatter.2
  249.5 62.4 all-gather.4
  324.0 76.5 reduce-scatter.4
  403.6 120.0 all-reduce.10
  529.7 157.4 all-reduce.8
where the time goes:
time: 710 us; the launch traced here: 701 us
  waiting for transfers between devices  369 us (52%)
  blocking collectives  97 us (14%)
  matrix products  88.4 us (12%)
  other arithmetic  70.4 us (10%)
  local copies, waits for them, and re-layouts  48.2 us (7%)
  between operations  16.4 us (2%)
  starting transfers between devices  11.6 us (2%)
    psum x1, waiting for transfers between devices, body(): lax.psum((grad_w_value, grad_b_value, grad_kernel, grad_w_out, grad_b_out...  89.3 us
    reduce_scatter x1, waiting for transfers between devices, body(): lax.psum_scatter(jnp.dot(active, w_down, preferred_element_type=jnp.float...  72.7 us
    reduce_scatter x1, waiting for transfers between devices, body(): lax.psum_scatter(dot_last(upper_grad, w_up).astype(jnp.bfloat16), 'tensor...  69.1 us
    psum x1, blocking collectives, body(): lax.psum((grad_w_value, grad_b_value, grad_kernel, grad_w_out, grad_b_out...  68.4 us
    all_gather x1, waiting for transfers between devices, body(): grad_rows_all = lax.all_gather(branch_grad, 'tensor', axis=0, tiled=True)  62.5 us
    dot_general x16, matrix products, dot_last(): lax.dot_general(former, latter, (((1,), (1,)), ((), ())), preferred_eleme...  56.4 us
    all_gather x1, waiting for transfers between devices, body(): gathered = lax.all_gather(first_low, 'tensor', axis=0, tiled=True)  53.2 us
    psum x1, blocking collectives, body(): lax.psum(grad_b_up.astype(jnp.bfloat16), 'dp').astype(jnp.float32)  28.5 us
  transfers between devices with their start and end apart: 6, of which 6 were waited for; matrix products, arithmetic and copies ran while one was open for 12% of the time, Pallas kernels for 0%

commit v1 on v0

--- a/solution.py
+++ b/solution.py
@@ -192,7 +192,7 @@
     grad_w_value = dot_first(block_input, value_grad)
     input_grad = resid_grad + dot_last(value_grad, w_value)
     grad_w_up, grad_w_down, grad_b_up = (
-        lax.psum(grad_w_up.astype(jnp.bfloat16), "dp").astype(jnp.float32),
+        jnp.sum(lax.all_gather(grad_w_up.astype(jnp.bfloat16), "dp"), axis=0).astype(jnp.float32),
         lax.psum(grad_w_down.astype(jnp.bfloat16), "dp").astype(jnp.float32),
         lax.psum(grad_b_up.astype(jnp.bfloat16), "dp").astype(jnp.float32),
     )

time: 710 us -> 770 us (1.085)
  waiting for transfers between devices: 369 us -> 413 us
  local copies, waits for them, and re-layouts: 48.2 us -> 72 us
  starting transfers between devices: 11.6 us -> 0.97 us
    all_gather x0 -> x1, waiting for transfers between devices: none -> 54.8 us  [body(): lax.all_gather(grad_w_up.astype(jnp.bfloat16), 'dp')]
    another operation x66, local copies, waits for them, and re-layouts: 25 us -> 48 us  [conv_back(): return (value_grad, jnp.stack(tap_rows, axis=0))]
    psum x1, waiting for transfers between devices: 22.6 us -> 0.01 us  [body(): lax.psum(grad_w_down.astype(jnp.bfloat16), 'dp').astype(jnp.float32)]
    all_gather x1, waiting for transfers between devices: 53.2 us -> 64 us  [body(): gathered = lax.all_gather(first_low, 'tensor', axis=0, tiled=True)]
    reduce_scatter x1, starting transfers between devices: 11.4 us -> 0.51 us  [body(): lax.psum_scatter(jnp.dot(active, w_down, preferred_element_type=jnp.float...]
    unnamed x253 -> x185, local copies, waits for them, and re-layouts: 16.1 us -> 16 us
  transfers between devices with their start and end apart: 6 -> 7, of which waited for: 6 -> 6; matrix products, arithmetic and copies ran while one was open for 12% -> 15% of each run, Pallas kernels for 0% -> 0%
where the time goes in v1:
time: 770 us; the launch traced here: 760 us
  waiting for transfers between devices  413 us (54%)
  blocking collectives  93.3 us (12%)
  matrix products  90.6 us (12%)
  other arithmetic  74.6 us (10%)
  local copies, waits for them, and re-layouts  72 us (9%)
  between operations  15.4 us (2%)
    psum x1, waiting for transfers between devices, body(): lax.psum((grad_w_value, grad_b_value, grad_kernel, grad_w_out, grad_b_out...  87.4 us
    reduce_scatter x1, waiting for transfers between devices, body(): lax.psum_scatter(jnp.dot(active, w_down, preferred_element_type=jnp.float...  72.8 us
    reduce_scatter x1, waiting for transfers between devices, body(): lax.psum_scatter(dot_last(upper_grad, w_up).astype(jnp.bfloat16), 'tensor...  71.9 us
    psum x1, blocking collectives, body(): lax.psum((grad_w_value, grad_b_value, grad_kernel, grad_w_out, grad_b_out...  64.9 us
    all_gather x1, waiting for transfers between devices, body(): gathered = lax.all_gather(first_low, 'tensor', axis=0, tiled=True)  64 us
    all_gather x1, waiting for transfers between devices, body(): grad_rows_all = lax.all_gather(branch_grad, 'tensor', axis=0, tiled=True)  62.5 us
    dot_general x16, matrix products, dot_last(): lax.dot_general(former, latter, (((1,), (1,)), ((), ())), preferred_eleme...  56.4 us
    all_gather x1, waiting for transfers between devices, body(): lax.all_gather(grad_w_up.astype(jnp.bfloat16), 'dp')  54.8 us
  transfers between devices with their start and end apart: 7, of which 6 were waited for; matrix products, arithmetic and copies ran while one was open for 15% of the time, Pallas kernels for 0%

profile of v1, /device:TPU:1, one launch (start us, length us, event | category | flops | bytes accessed | tf_op | source)
XLA Modules:
  0.0 760.3 jit_solution(16098554532656479387)
XLA Ops:
  17.3 43.1 %while.12 = (s32[]{:T(128)}, bf16[12,256,256]{2,1,0:T(8,128)(2,1)}, s32[12,256,32]{1,2,0:T(8,128)S(1)}, s32[12,256,32]{1,2,0:T(8,128)S(1)}, s32[256]{0:T(256)S(1)}, /*index=5*/s32[]{:T(128)}) while((s32[]{:T(128)}, bf16[12,256,256]{2,1,0:T(8,128)(2,1)}, s32[12,256,32]{1,2,0:T(8,128)S(1)}, s32[12,256,32]{1,2,0:T(8,128)S(1)}, ...), condition=%wide.region_3.4_spmd.clone.clone, body=%wide.region_2.3_spmd.clone.clone.sunk | while | flops 1078198272 | bytes 330313 | solution.py:125
  17.4 3.6 fusion.266
  24.5 3.6 fusion.266
  31.7 3.6 fusion.266
  35.3 3.6 fusion.266
  42.5 3.6 fusion.266
  49.7 3.6 fusion.266
  56.8 3.6 fusion.266
  66.2 11.6 %add_convert_fusion.2 = bf16[256,768]{1,0:T(8,128)(2,1)S(1)} fusion(f32[256,768]{1,0:T(8,128)S(1)} %copy.51, f32[256,768]{1,0:T(8,128)S(1)} %get-tuple-element.366, f32[768]{0:T(1024)} %get-tuple-element.198, f32[256]{0:T(256)} %get-tuple-element.364, f32[768]{0:T(1024)} %get-tuple-element.199, f32[256]{0:T(256)} %get-tuple-element.363, ...), kind=kLoop, calls=%fused_computation.456 | loop fusion | flops 38338560 | bytes 2231296 | tf_op jit(solution)/shard_map/convert_element_type | solution.py:140
  85.3 64.0 %all-gather.5.cloned.1.call-done = bf16[2048,768]{1,0:T(8,128)(2,1)} async-done(((bf16[256,768]{1,0:T(8,128)(2,1)}), bf16[2048,768]{1,0:T(8,128)(2,1)}) %all-gather.5.cloned.1.call-update) | async-done | bytes 3145744 | tf_op jit(solution)/shard_map/all_gather | solution.py:151
  149.3 11.6 %multiply_convert_fusion = (bf16[2048,384]{1,0:T(8,128)(2,1)S(1)}, f32[2048,384]{1,0:T(8,128)}, f32[2048,384]{1,0:T(8,128)}) fusion(f32[384]{0:T(512)} %convert_element_type.531, bf16[2048,768]{1,0:T(8,128)(2,1)} %all-gather.5.cloned.1.call-done, bf16[768,384]{1,0:T(8,128)(2,1)} %param.29), kind=kOutput, calls=%fused_computation.148 | convolution fusion | flops 1259864064 | bytes 11601408 | tf_op jit(solution)/shard_map/dot_general | solution.py:152
  169.4 72.8 %reduce-scatter.3.cloned.1.call-done = bf16[256,768]{1,0:T(8,128)(2,1)} async-done(((bf16[2048,768]{1,0:T(8,128)(2,1)}), bf16[256,768]{1,0:T(8,128)(2,1)}) %reduce-scatter.3.cloned.1.call-update) | async-done | bytes 393232 | tf_op jit(solution)/shard_map/reduce_scatter | solution.py:155
  249.3 62.5 %all-gather.7.cloned.1.call-done = bf16[2048,768]{1,0:T(8,128)(2,1)} async-done(((bf16[256,768]{1,0:T(8,128)(2,1)}), bf16[2048,768]{1,0:T(8,128)(2,1)}) %all-gather.7.cloned.1.call-update) | async-done | bytes 3145744 | tf_op jit(solution)/shard_map/all_gather | solution.py:167
  311.8 7.3 fusion.230
  323.9 4.6 convolution_convert_fusion.2
  328.5 71.9 %reduce-scatter.5.cloned.1.call-done = bf16[256,768]{1,0:T(8,128)(2,1)} async-done(((bf16[2048,768]{1,0:T(8,128)(2,1)}), bf16[256,768]{1,0:T(8,128)(2,1)}) %reduce-scatter.5.cloned.1.call-update) | async-done | bytes 393232 | tf_op jit(solution)/shard_map/reduce_scatter | solution.py:173
  431.1 11.7 %convert_reduce_fusion.3 = (f32[768]{0:T(1024)S(1)}, bf16[256,768]{1,0:T(8,128)(2,1)S(1)}) fusion(f32[256]{0:T(256)} %copy-done.76, f32[256,768]{1,0:T(8,128)} %copy.53, f32[768]{0:T(1024)} %get-tuple-element.198, f32[256]{0:T(256)} %get-tuple-element.301, f32[768]{0:T(1024)} %get-tuple-element.199, f32[256]{0:T(256)} %get-tuple-element.319, ...), kind=kLoop, calls=%fused_computation.446 | loop fusion | flops 38927616 | bytes 2235392 | tf_op jit(solution)/shard_map/reduce_sum | solution.py:191
  485.1 5.8 stack.263
  495.2 5.0 convolution_convert_fusion.3
  500.2 28.4 %psum.91 = bf16[384]{0:T(512)(128)(2,1)S(1)} all-reduce(bf16[384]{0:T(512)(128)(2,1)S(1)} %copy-done.86), channel_id=1, replica_groups=mesh['dp'=16,'tensor'=8] {'dp'}, use_global_device_ids=true, to_apply=%region_94.95 | all-reduce | flops 384 | bytes 1536 | tf_op jit(solution)/shard_map/psum | solution.py:197
  531.4 64.9 %all-reduce.3 = (f32[768]{0:T(1024)}, f32[768]{0:T(1024)}, f32[768]{0:T(1024)}, f32[768]{0:T(1024)}, f32[768]{0:T(1024)}, /*index=5*/f32[768]{0:T(1024)}, f32[768]{0:T(1024)}) all-reduce(f32[768]{0:T(1024)S(1)} %get-tuple-element.288, f32[768]{0:T(1024)S(1)} %copy-done.37, ...), channel_id=1, replica_groups=mesh['dp'=16,'tensor'=8] {'dp','tensor'}, use_global_device_ids=true, to_apply=%region_18.19 | all-reduce | flops 5376 | bytes 43008 | tf_op jit(solution)/shard_map/psum | solution.py:210
  597.7 87.4 %all-reduce.10.cloned.1.call-done = (f32[768,768]{0,1:T(8,128)}, f32[65,768]{1,0:T(8,128)}, f32[768,768]{1,0:T(8,128)}) async-done(((f32[768,768]{0,1:T(8,128)}, f32[65,768]{1,0:T(8,128)}, f32[768,768]{1,0:T(8,128)}), (f32[768,768]{0,1:T(8,128)}, f32[65,768]{1,0:T(8,128)}, f32[768,768]{1,0:T(8,128)})) %all-reduce.10.cloned.1.call-update) | async-done | bytes 4918288 | tf_op jit(solution)/shard_map/psum | solution.py:210
  688.1 54.8 %all-gather.9.cloned.1.call-done = bf16[12288,384]{1,0:T(8,128)(2,1)} async-done(((bf16[768,384]{1,0:T(8,128)(2,1)}), bf16[12288,384]{1,0:T(8,128)(2,1)}) %all-gather.9.cloned.1.call-update) | async-done | bytes 9437200 | tf_op jit(solution)/shard_map/all_gather | solution.py:195
  742.9 5.4 reduce_sum.887
  (349 shorter events, 150.1 us)
Async XLA Ops:
  7.2 53.3 %copy-start = (bf16[768,768]{1,0:T(8,128)(2,1)S(1)}, bf16[768,768]{1,0:T(8,128)(2,1)}, u32[]{:S(2)}) copy-start(bf16[768,768]{1,0:T(8,128)(2,1)} %param.22) | copy-start | bytes 3538948
  7.2 142.1 %all-gather.5.cloned.1.call-start = ((), (), s32[]{:S(2)}) async-start(), calls=%async_computation.2 | async-start | bytes 3538944 | tf_op jit(solution)/shard_map/all_gather | solution.py:151
  17.3 43.1 %copy-start.85 = (s32[256]{0:T(256)S(1)}, s32[256]{0:T(256)}, u32[]{:S(2)}) copy-start(s32[256]{0:T(256)} %param.37) | copy-start | bytes 3076
  17.3 43.1 %copy-start.82 = (bf16[768]{0:T(1024)(128)(2,1)S(1)}, bf16[768]{0:T(1024)(128)(2,1)}, u32[]{:S(2)}) copy-start(bf16[768]{0:T(1024)(128)(2,1)} %param.23) | copy-start | bytes 4612
  17.3 43.1 %copy-start.6 = (bf16[256,768]{1,0:T(8,128)(2,1)S(1)}, bf16[256,768]{1,0:T(8,128)(2,1)}, u32[]{:S(2)}) copy-start(bf16[256,768]{1,0:T(8,128)(2,1)} %param.21) | copy-start | bytes 1179652
  83.5 158.6 %reduce-scatter.3.cloned.1.call-start = ((), (), s32[]{:S(2)}) async-start(), calls=%async_computation.3 | async-start | bytes 3538944 | tf_op jit(solution)/shard_map/reduce_scatter | solution.py:155
  165.5 146.3 %all-gather.7.cloned.1.call-start = ((), (), s32[]{:S(2)}) async-start(), calls=%async_computation.4 | async-start | bytes 3538944 | tf_op jit(solution)/shard_map/all_gather | solution.py:167
  249.3 151.2 %reduce-scatter.5.cloned.1.call-start = ((), (), s32[]{:S(2)}) async-start(), calls=%async_computation.5 | async-start | bytes 3538944 | tf_op jit(solution)/shard_map/reduce_scatter | solution.py:173
  323.8 205.4 %all-reduce.8.cloned.1.call-start = ((), (), s32[]{:S(2)}) async-start(), calls=%async_computation.6 | async-start | bytes 1179648 | tf_op jit(solution)/shard_map/psum | solution.py:196
  328.5 356.6 %all-reduce.10.cloned.1.call-start = ((), (), s32[]{:S(2)}) async-start(), calls=%async_computation.8 | async-start | bytes 9879552 | tf_op jit(solution)/shard_map/psum | solution.py:210
  428.7 55.0 %copy-start.40 = (f32[768]{0:T(1024)S(1)}, f32[768]{0:T(1024)}, u32[]{:S(2)}) copy-start(f32[768]{0:T(1024)} %get-tuple-element.184) | copy-start | bytes 9220
  428.8 55.0 %copy-start.39 = (f32[768]{0:T(1024)S(1)}, f32[768]{0:T(1024)}, u32[]{:S(2)}) copy-start(f32[768]{0:T(1024)} %get-tuple-element.183) | copy-start | bytes 9220
  428.8 55.0 %copy-start.38 = (f32[768]{0:T(1024)S(1)}, f32[768]{0:T(1024)}, u32[]{:S(2)}) copy-start(f32[768]{0:T(1024)} %get-tuple-element.182) | copy-start | bytes 9220
  428.8 62.2 %copy-start.9 = (bf16[256,768]{1,0:T(8,128)(2,1)S(1)}, bf16[256,768]{1,0:T(8,128)(2,1)}, u32[]{:S(2)}) copy-start(bf16[256,768]{1,0:T(8,128)(2,1)} %copy-done.8) | copy-start | bytes 1179652
  428.8 62.2 %copy-start.12 = (bf16[256,768]{1,0:T(8,128)(2,1)S(1)}, bf16[256,768]{1,0:T(8,128)(2,1)}, u32[]{:S(2)}) copy-start(bf16[256,768]{1,0:T(8,128)(2,1)} %copy-done.11) | copy-start | bytes 1179652
  431.1 61.7 %copy-start.7 = (bf16[256,768]{1,0:T(8,128)(2,1)S(1)}, bf16[256,768]{1,0:T(8,128)(2,1)}, u32[]{:S(2)}) copy-start(bf16[256,768]{1,0:T(8,128)(2,1)} %param.21) | copy-start | bytes 1179652
  494.8 36.5 %copy-start.32 = (f32[768]{0:T(1024)S(1)}, f32[768]{0:T(1024)}, u32[]{:S(2)}) copy-start(f32[768]{0:T(1024)} %get-tuple-element.193) | copy-start | bytes 9220
  494.8 36.5 %copy-start.33 = (f32[768]{0:T(1024)S(1)}, f32[768]{0:T(1024)}, u32[]{:S(2)}) copy-start(f32[768]{0:T(1024)} %get-tuple-element.196) | copy-start | bytes 9220
  494.8 36.5 %copy-start.34 = (f32[768]{0:T(1024)S(1)}, f32[768]{0:T(1024)}, u32[]{:S(2)}) copy-start(f32[768]{0:T(1024)} %get-tuple-element.284) | copy-start | bytes 9220
  494.9 36.5 %copy-start.35 = (f32[768]{0:T(1024)S(1)}, f32[768]{0:T(1024)}, u32[]{:S(2)}) copy-start(f32[768]{0:T(1024)} %get-tuple-element.126) | copy-start | bytes 9220
  494.9 36.5 %copy-start.36 = (f32[768]{0:T(1024)S(1)}, f32[768]{0:T(1024)}, u32[]{:S(2)}) copy-start(f32[768]{0:T(1024)} %get-tuple-element.195) | copy-start | bytes 9220
  494.9 101.4 %copy-start.3 = (f32[256,768]{1,0:T(8,128)S(1)}, f32[256,768]{1,0:T(8,128)}, u32[]{:S(2)}) copy-start(f32[256,768]{1,0:T(8,128)} %copy-done.2) | copy-start | bytes 2359300
  494.9 101.4 %copy-start.81 = (f32[256]{0:T(256)S(1)}, f32[256]{0:T(256)}, u32[]{:S(2)}) copy-start(f32[256]{0:T(256)} %copy-done.80) | copy-start | bytes 3076
  494.9 248.0 %all-gather.9.cloned.1.call-start = ((), (), s32[]{:S(2)}) async-start(), calls=%async_computation.7 | async-start | bytes 10027008 | tf_op jit(solution)/shard_map/all_gather | solution.py:195
  (73 other events, 520.0 us)
Sparse Core Ops, SparseCore 0:
  83.6 65.6 all-gather.4
  165.6 76.4 reduce-scatter.2
  249.4 62.3 all-gather.6
  323.9 76.4 reduce-scatter.4
  402.8 115.1 all-reduce.7
  524.9 160.1 all-reduce.9
  686.7 56.1 all-gather.8
